TPU v7x, 32 devices: a whole 2x2x4 slice. The times are simulated.
32 devices in a mesh: dp: 16 (over z, x, core), rows: 2 (over y).
Axes of the slice: x: 2, y: 2, z: 4, core: 2. Of those that a mesh axis runs over, the one named last changes fastest.
Arguments:
- features: bfloat16 [32, 12, 64, 1024], P('dp', 'rows'), may hold values from -8 to 8
- first_atrous_weight: bfloat16 [3, 3, 1024, 256], P(None, None, 'dp'), may hold values from -0.0625 to 0.0625
- second_atrous_weight: bfloat16 [3, 3, 1024, 256], P(None, None, 'dp'), may hold values from -0.0625 to 0.0625
- third_atrous_weight: bfloat16 [3, 3, 1024, 256], P(None, None, 'dp'), may hold values from -0.0625 to 0.0625
- pointwise_weight: bfloat16 [1024, 256], replicated, may hold values from -0.1875 to 0.1875
- pooling_weight: bfloat16 [1024, 256], replicated, may hold values from -0.1875 to 0.1875
- projection_weight: bfloat16 [1280, 256], replicated, may hold values from -0.15625 to 0.15625
- branch_norm_gain: float32 [4, 256], replicated, may hold values from 0.25 to 1.75
- branch_norm_shift: float32 [4, 256], replicated, may hold values from -3 to 3
- projection_norm_gain: float32 [256], replicated, may hold values from 0.25 to 1.75
- projection_norm_shift: float32 [256], replicated, may hold values from -3 to 3
- ghost_group_index: int32 [32], replicated, may hold values from 0 to 7, as said below
Outputs:
- decoder_in: bfloat16 [32, 12, 64, 256], P(None, 'rows', 'dp')
Inputs may be any that keep to these rules, and one draw needn't show every extreme that they name: `ghost_group_index`: each of the 8 group ids names exactly 4 images.
All inputs are finite; a program needn't handle non-finite values.
Results may differ from a plain program's by a relative error of at most 0.0014.
The roundings to bfloat16 on the way count: a program that leaves them out, or rounds other values in their place, can miss the bound.
Values may be sent and summed in bfloat16 or wider, within the bound.
No kernel may reach another device: no remote copies, remote signals or barrier semaphores. Data moves between devices by JAX's collectives and lax.ppermute only.
A program may use at most 128 MiB of HBM per device.

v0:
```python
import jax
import jax.numpy as jnp
from jax import lax
from jax.sharding import PartitionSpec as P

DILATION_FIRST = 12
DILATION_SECOND = 24
DILATION_THIRD = 36


def from_behind(array, axis, by):
    count = lax.axis_size(axis)
    pairs = [(i, i + by) for i in range(count) if 0 <= i + by < count]
    return lax.ppermute(array, axis, pairs)


def row_tap_list(block_tensor, kernel_row_slice, dilation_rate):
    partial_terms = jnp.einsum(
        "irwc,kco->irwko", block_tensor, kernel_row_slice, preferred_element_type=jnp.float32
    )
    map_width = block_tensor.shape[2]
    left_padding = jnp.pad(partial_terms[:, :, :, 0], ((0, 0), (0, 0), (dilation_rate, 0), (0, 0)))[
        :, :, :map_width
    ]
    right_padding = jnp.pad(
        partial_terms[:, :, :, 2], ((0, 0), (0, 0), (0, dilation_rate), (0, 0))
    )[:, :, dilation_rate:]
    return partial_terms[:, :, :, 1] + left_padding + right_padding


def dilated_result(features, kernel_weight, dilation_rate):
    step_offsets = dilation_rate // features.shape[1]
    running_sum = row_tap_list(features, kernel_weight[1], dilation_rate)
    for by_dev, tap_offset in ((step_offsets, 0), (-step_offsets, 2)):
        partial_taps = row_tap_list(features, kernel_weight[tap_offset], dilation_rate)
        running_sum = running_sum + from_behind(partial_taps, "rows", by_dev)
    return running_sum


def stats_terms(pre, onehot):
    first = jnp.sum(pre, axis=(1, 2))
    second = jnp.sum(pre * pre, axis=(1, 2))
    group_first = jnp.dot(onehot.T, first, precision=lax.Precision.HIGHEST)
    group_second = jnp.dot(onehot.T, second, precision=lax.Precision.HIGHEST)
    return (group_first, group_second)


def apply_norm(pre, onehot, total_first, total_second, count, gain, shift):
    mean = total_first / count
    var = total_second / count - mean * mean
    inv = lax.rsqrt(var + 1e-05)
    img_mean = jnp.dot(onehot, mean, precision=lax.Precision.HIGHEST)
    img_inv = jnp.dot(onehot, inv, precision=lax.Precision.HIGHEST)
    scaled = (pre - img_mean[:, None, None, :]) * img_inv[:, None, None, :] * gain + shift
    return jax.nn.relu(scaled).astype(jnp.bfloat16)


def project(joined, onehot, projection_weight, count, projection_norm_gain, projection_norm_shift):
    proj = jnp.einsum(
        "irwc,co->irwo", joined, projection_weight, preferred_element_type=jnp.float32
    )
    group_first, group_second = stats_terms(proj, onehot)
    total_first, total_second = lax.psum((group_first, group_second), ("dp", "rows"))
    return apply_norm(
        proj, onehot, total_first, total_second, count, projection_norm_gain, projection_norm_shift
    )


def shards(
    features,
    first_atrous_weight,
    second_atrous_weight,
    third_atrous_weight,
    pointwise_weight,
    pooling_weight,
    projection_weight,
    branch_norm_gain,
    branch_norm_shift,
    projection_norm_gain,
    projection_norm_shift,
    ghost_group_index,
):
    img_dev, rows_dev, cols, chans = features.shape
    dp_size = lax.axis_size("dp")
    rows_size = lax.axis_size("rows")
    images = img_dev * dp_size
    groups = images // 4
    pixels = rows_dev * rows_size * cols
    count = 4.0 * pixels
    start = lax.axis_index("dp") * img_dev
    labels = jnp.arange(groups, dtype=jnp.int32)
    all_hot = (ghost_group_index[:, None] == labels[None, :]).astype(jnp.float32)
    own_hot = lax.dynamic_slice_in_dim(all_hot, start, img_dev, 0)
    first_kernel, second_kernel, third_kernel = (
        lax.all_gather(first_atrous_weight, "dp", axis=2, tiled=True),
        lax.all_gather(second_atrous_weight, "dp", axis=2, tiled=True),
        lax.all_gather(third_atrous_weight, "dp", axis=2, tiled=True),
    )
    pointwise_output = jnp.einsum(
        "irwc,co->irwo", features, pointwise_weight, preferred_element_type=jnp.float32
    )
    pre = jnp.concatenate(
        [
            pointwise_output,
            dilated_result(features, first_kernel, DILATION_FIRST),
            dilated_result(features, second_kernel, DILATION_SECOND),
            dilated_result(features, third_kernel, DILATION_THIRD),
        ],
        -1,
    )
    group_first, group_second = stats_terms(pre, own_hot)
    pool_part = jnp.sum(features, axis=(1, 2), dtype=jnp.float32)
    pool_total = lax.psum(pool_part, "rows")
    total_first, total_second = lax.psum((group_first, group_second), ("dp", "rows"))
    branches = apply_norm(
        pre,
        own_hot,
        total_first,
        total_second,
        count,
        branch_norm_gain.reshape(-1),
        branch_norm_shift.reshape(-1),
    )
    pooled = (pool_total / pixels).astype(jnp.bfloat16)
    pool_act = jax.nn.relu(
        jnp.dot(pooled, pooling_weight, preferred_element_type=jnp.float32)
    ).astype(jnp.bfloat16)
    pool_map = jnp.broadcast_to(
        pool_act[:, None, None, :], (img_dev, rows_dev, cols, pool_act.shape[1])
    )
    joined = jnp.concatenate([branches, pool_map], -1)
    local_out = project(
        joined, own_hot, projection_weight, count, projection_norm_gain, projection_norm_shift
    )
    return lax.all_to_all(local_out, "dp", split_axis=2, concat_axis=0, tiled=True)


def solution(mesh):
    in_specs = (
        P("dp", "rows", None, None),
        P(None, None, "dp", None),
        P(None, None, "dp", None),
        P(None, None, "dp", None),
        P(),
        P(),
        P(),
        P(),
        P(),
        P(),
        P(),
        P(),
    )
    out_specs = P(None, "rows", "dp", None)
    return jax.shard_map(shards, mesh=mesh, in_specs=in_specs, out_specs=out_specs, check_vma=False)
```

profile of v0, /device:TPU:0, one launch (start us, length us, event | category | flops | bytes accessed | tf_op | source)
XLA Modules:
  0.0 381.6 jit_solution(11481842989761349140)
XLA Ops:
  6.5 0.7 all-gather.4.cloned.1.call-update
  7.3 0.7 all-gather.6.cloned.1.call-update
  8.1 0.7 all-gather.8.cloned.1.call-update
  8.8 0.7 dynamic-slice
  9.5 1.7 convert_reduce_fusion
  11.2 6.0 %psum.37 = f32[2,1024]{1,0:T(2,128)S(1)} all-reduce(f32[2,1024]{1,0:T(2,128)S(1)} %convert_reduce_fusion), channel_id=1, replica_groups=mesh['dp'=16,'rows'=2] {'rows'}, use_global_device_ids=true, to_apply=%region_5.6 | all-reduce | flops 2048 | bytes 16384 | tf_op jit(solution)/shard_map/psum | solution.py:113
  17.2 1.5 fusion.49
  18.7 46.5 %all-gather.4.cloned.1.call-done = bf16[3,3,1024,256]{3,2,1,0:T(8,128)(2,1)} async-done(((bf16[3,3,64,256]{3,2,1,0:T(8,128)(2,1)}), bf16[3,3,1024,256]{3,2,1,0:T(8,128)(2,1)}) %all-gather.4.cloned.1.call-update) | async-done | bytes 4718608 | tf_op jit(solution)/shard_map/all_gather | solution.py:95
  65.2 2.8 fusion.11
  68.0 0.1 slice_bitcast_fusion.39
  68.1 1.0 fusion.28
  69.2 1.5 collective-permute-start
  70.7 2.8 fusion.10
  73.5 0.1 slice_bitcast_fusion.36
  73.6 1.1 fusion.30
  74.7 1.5 collective-permute-start.1
  76.2 42.7 %all-gather.6.cloned.1.call-done = bf16[3,3,1024,256]{3,2,1,0:T(8,128)(2,1)} async-done(((bf16[3,3,64,256]{3,2,1,0:T(8,128)(2,1)}), bf16[3,3,1024,256]{3,2,1,0:T(8,128)(2,1)}) %all-gather.6.cloned.1.call-update) | async-done | bytes 4718608 | tf_op jit(solution)/shard_map/all_gather | solution.py:96
  119.0 2.8 fusion.8
  121.7 0.1 slice_bitcast_fusion.30
  121.9 1.0 fusion.36
  122.9 1.6 collective-permute-start.2
  124.4 2.8 fusion.7
  127.2 0.1 slice_bitcast_fusion.27
  127.3 1.0 fusion.38
  128.3 1.5 collective-permute-start.3
  129.9 2.8 fusion.12
  132.7 1.4 copy-done.4
  134.1 1.0 slice_bitcast_fusion.42
  135.1 37.6 %all-gather.8.cloned.1.call-done = bf16[3,3,1024,256]{3,2,1,0:T(8,128)(2,1)} async-done(((bf16[3,3,64,256]{3,2,1,0:T(8,128)(2,1)}), bf16[3,3,1024,256]{3,2,1,0:T(8,128)(2,1)}) %all-gather.8.cloned.1.call-update) | async-done | bytes 4718608 | tf_op jit(solution)/shard_map/all_gather | solution.py:97
  172.7 2.8 fusion.5
  175.5 0.1 slice_bitcast_fusion.21
  175.6 0.1 fusion.44
  175.7 1.0 collective-permute-start.4
  176.8 3.0 fusion.9
  179.8 1.4 fusion.4
  181.2 1.4 fusion.6
  182.6 0.1 slice_bitcast_fusion.33
  182.9 0.1 fusion.46
  183.0 0.8 collective-permute-start.5
  183.9 0.1 slice_bitcast_fusion.24
  184.0 0.1 copy-done.3
  184.1 1.9 fusion.26
  186.0 1.6 fusion.34
  187.7 0.2 fusion.42
  187.9 0.9 copy-done.1
  188.8 0.4 fusion.48
  189.2 0.9 fusion.79
  190.1 0.9 fusion.78
  191.0 0.2 fusion.22
  191.2 0.7 copy.120
  191.9 117.9 %all-reduce.22.cloned.1.call-done = (f32[8,1024]{1,0:T(8,128)}, f32[8,1024]{1,0:T(8,128)}) async-done(((f32[8,1024]{1,0:T(8,128)}, f32[8,1024]{1,0:T(8,128)}), (f32[8,1024]{1,0:T(8,128)}, f32[8,1024]{1,0:T(8,128)})) %all-reduce.22.cloned.1.call-update) | async-done | bytes 65552 | tf_op jit(solution)/shard_map/psum | solution.py:114
  309.8 1.0 fusion.58
  310.7 1.0 fusion.51
  311.7 1.7 maximum_convert_fusion
  313.5 0.7 fusion.96
  314.2 0.3 fusion.77
  314.5 0.3 fusion.76
  314.7 41.1 %all-reduce.18 = (f32[8,256]{1,0:T(8,128)S(1)}, f32[8,256]{1,0:T(8,128)S(1)}) all-reduce(f32[8,256]{1,0:T(8,128)S(1)} %fusion.76, f32[8,256]{1,0:T(8,128)S(1)} %fusion.77), channel_id=1, replica_groups=mesh['dp'=16,'rows'=2] {'dp','rows'}, use_global_device_ids=true, to_apply=%region_9.10 | all-reduce | flops 4096 | bytes 32768 | tf_op jit(solution)/shard_map/psum | solution.py:63
  355.8 0.2 fusion.70
  356.0 0.2 fusion.63
  356.2 0.1 maximum_convert_fusion.1
  356.4 0.4 copy.97
  356.8 17.3 %all_to_all.18 = bf16[2,6,64,256]{3,0,1,2:T(2,128)(2,1)S(1)} all-to-all(bf16[2,6,64,256]{3,0,1,2:T(2,128)(2,1)S(1)} %copy.97), channel_id=1, replica_groups=mesh['dp'=16,'rows'=2] {'dp'}, dimensions={2} | all-to-all | bytes 786432 | tf_op jit(solution)/shard_map/all_to_all | solution.py:135
  374.1 0.9 copy.98
  (40 shorter events, 0.4 us)
Async XLA Ops:
  6.5 306.9 %copy-start = (bf16[1280,256]{1,0:T(8,128)(2,1)S(1)}, bf16[1280,256]{1,0:T(8,128)(2,1)}, u32[]{:S(2)}) copy-start(bf16[1280,256]{1,0:T(8,128)(2,1)} %param.18) | copy-start | bytes 1966084
  6.5 10.7 %copy-start.2 = (bf16[2,6,64,1024]{3,2,1,0:T(8,128)(2,1)S(1)}, bf16[2,6,64,1024]{3,2,1,0:T(8,128)(2,1)}, u32[]{:S(2)}) copy-start(bf16[2,6,64,1024]{3,2,1,0:T(8,128)(2,1)} %param.12) | copy-start | bytes 4718596
  6.5 10.7 %copy-start.6 = (bf16[1024,256]{1,0:T(8,128)(2,1)S(1)}, bf16[1024,256]{1,0:T(8,128)(2,1)}, u32[]{:S(2)}) copy-start(bf16[1024,256]{1,0:T(8,128)(2,1)} %param.16) | copy-start | bytes 1572868
  6.5 58.7 %all-gather.4.cloned.1.call-start = ((), (), s32[]{:S(2)}) async-start(), calls=%async_computation.1 | async-start | bytes 5013504 | tf_op jit(solution)/shard_map/all_gather | solution.py:95
  7.3 111.7 %all-gather.6.cloned.1.call-start = ((), (), s32[]{:S(2)}) async-start(), calls=%async_computation.2 | async-start | bytes 5013504 | tf_op jit(solution)/shard_map/all_gather | solution.py:96
  8.0 164.7 %all-gather.8.cloned.1.call-start = ((), (), s32[]{:S(2)}) async-start(), calls=%async_computation.3 | async-start | bytes 5013504 | tf_op jit(solution)/shard_map/all_gather | solution.py:97
  8.7 301.0 %all-reduce.22.cloned.1.call-start = ((), (), s32[]{:S(2)}) async-start(), calls=%async_computation.4 | async-start | bytes 131072 | tf_op jit(solution)/shard_map/psum | solution.py:114
  9.5 180.5 %copy-start.10 = (s32[2]{0:T(128)}, s32[2]{0:T(128)S(1)}, u32[]{:S(2)}) copy-start(s32[2]{0:T(128)S(1)} %dynamic-slice) | copy-start | bytes 28
  69.2 113.8 %collective-permute-start = (f32[2,6,64,256]{3,2,1,0:T(8,128)}, f32[2,6,64,256]{3,2,1,0:T(8,128)}, u32[]{:S(2)}, u32[]{:S(2)}) collective-permute-start(f32[2,6,64,256]{3,2,1,0:T(8,128)} %fusion.28), channel_id=1, source_target_pairs={} | collective-permute-start | bytes 2359304 | tf_op jit(solution)/shard_map/ppermute | solution.py:14
  74.7 109.3 %collective-permute-start.1 = (f32[2,6,64,256]{3,2,1,0:T(8,128)}, f32[2,6,64,256]{3,2,1,0:T(8,128)}, u32[]{:S(2)}, u32[]{:S(2)}) collective-permute-start(f32[2,6,64,256]{3,2,1,0:T(8,128)} %fusion.30), channel_id=1, source_target_pairs={} | collective-permute-start | bytes 2359304 | tf_op jit(solution)/shard_map/ppermute | solution.py:14
  122.9 63.2 %collective-permute-start.2 = (f32[2,6,64,256]{3,2,1,0:T(8,128)}, f32[2,6,64,256]{3,2,1,0:T(8,128)}, u32[]{:S(2)}, u32[]{:S(2)}) collective-permute-start(f32[2,6,64,256]{3,2,1,0:T(8,128)} %fusion.36), channel_id=1, source_target_pairs={} | collective-permute-start | bytes 2359304 | tf_op jit(solution)/shard_map/ppermute | solution.py:14
  128.3 57.7 %collective-permute-start.3 = (f32[2,6,64,256]{3,2,1,0:T(8,128)}, f32[2,6,64,256]{3,2,1,0:T(8,128)}, u32[]{:S(2)}, u32[]{:S(2)}) collective-permute-start(f32[2,6,64,256]{3,2,1,0:T(8,128)} %fusion.38), channel_id=1, source_target_pairs={} | collective-permute-start | bytes 2359304 | tf_op jit(solution)/shard_map/ppermute | solution.py:14
  132.7 1.4 copy-start.4
  175.6 4.2 %slice-start = ((s8[4718592]{0:T(1024)(128)(4,1)}), s8[4194304]{0:T(1024)(128)(4,1)S(1)}, s32[]{:S(2)}) async-start(s8[4718592]{0:T(1024)(128)(4,1)} %bitcast.185), calls=%async_computation.5 | async-start | bytes 8388608
  175.7 4.1 %slice-start.1 = ((s8[4718592]{0:T(1024)(128)(4,1)}), s8[524288]{0:T(1024)(128)(4,1)S(1)}, s32[]{:S(2)}) async-start(s8[4718592]{0:T(1024)(128)(4,1)} %bitcast.185), calls=%async_computation.6 | async-start | bytes 1048576
  175.7 11.9 %collective-permute-start.4 = (f32[2,6,64,256]{3,2,1,0:T(8,128)S(1)}, f32[2,6,64,256]{3,2,1,0:T(8,128)S(1)}, u32[]{:S(2)}, u32[]{:S(2)}) collective-permute-start(f32[2,6,64,256]{3,2,1,0:T(8,128)S(1)} %fusion.44), channel_id=1, source_target_pairs={} | collective-permute-start | bytes 2359304 | tf_op jit(solution)/shard_map/ppermute | solution.py:14
  183.0 1.1 copy-start.3
  183.0 4.6 %collective-permute-start.5 = (f32[2,6,64,256]{3,2,1,0:T(8,128)S(1)}, f32[2,6,64,256]{3,2,1,0:T(8,128)S(1)}, u32[]{:S(2)}, u32[]{:S(2)}) collective-permute-start(f32[2,6,64,256]{3,2,1,0:T(8,128)S(1)} %fusion.46), channel_id=1, source_target_pairs={} | collective-permute-start | bytes 2359304 | tf_op jit(solution)/shard_map/ppermute | solution.py:14
  187.7 1.1 copy-start.1
  188.8 2.2 copy-start.5
  188.8 2.4 copy-start.7
  313.5 0.7 copy-start.11
  313.5 42.7 %copy-start.8 = (f32[256]{0:T(256)S(1)}, f32[256]{0:T(256)}, u32[]{:S(2)}) copy-start(f32[256]{0:T(256)} %param.22) | copy-start | bytes 3076
  313.5 42.7 %copy-start.9 = (f32[256]{0:T(256)S(1)}, f32[256]{0:T(256)}, u32[]{:S(2)}) copy-start(f32[256]{0:T(256)} %param.21) | copy-start | bytes 3076
Sparse Core Ops, SparseCore 0:
  9.5 55.6 all-gather.3
  67.4 51.4 all-gather.5
  121.1 51.4 all-gather.7
  191.1 118.6 all-reduce.21
where the time goes:
time: 382 us
  waiting for transfers between devices  247 us (65%)
  blocking collectives  64.4 us (17%)
  matrix products  29.5 us (8%)
  between operations  13.5 us (4%)
  other arithmetic  12 us (3%)
  starting transfers between devices  8.15 us (2%)
  local copies, waits for them, and re-layouts  7.13 us (2%)
    psum x1, waiting for transfers between devices, shards(): lax.psum((group_first, group_second), ('dp', 'rows'))  118 us
    all_gather x1, waiting for transfers between devices, shards(): lax.all_gather(first_atrous_weight, 'dp', axis=2, tiled=True)  46.5 us
    all_gather x1, waiting for transfers between devices, shards(): lax.all_gather(second_atrous_weight, 'dp', axis=2, tiled=True)  42.7 us
    psum x1, blocking collectives, project(): lax.psum((group_first, group_second), ('dp', 'rows'))  41.1 us
    all_gather x1, waiting for transfers between devices, shards(): lax.all_gather(third_atrous_weight, 'dp', axis=2, tiled=True)  37.6 us
    dot_general x9, matrix products, row_tap_list(): jnp.einsum('irwc,kco->irwko', block_tensor, kernel_row_slice, preferred_e...  22.5 us
    all_to_all x1, blocking collectives, shards(): lax.all_to_all(local_out, 'dp', split_axis=2, concat_axis=0, tiled=True)  17.3 us
    ppermute x6, starting transfers between devices, from_behind(): return lax.ppermute(array, axis, pairs)  8.03 us
  transfers between devices with their start and end apart: 10, of which 4 were waited for; matrix products, arithmetic and copies ran while one was open for 10% of the time, Pallas kernels for 0%

commit v1 on v0

--- a/solution.py
+++ b/solution.py
@@ -6,6 +6,28 @@
 DILATION_FIRST = 12
 DILATION_SECOND = 24
 DILATION_THIRD = 36
+
+
+def in_order(pieces, dim):
+    lengths = list(pieces.shape[1:])
+    lengths[dim] *= pieces.shape[0]
+    return jnp.moveaxis(pieces, 0, dim).reshape(lengths)
+
+
+def ring_gather(x, axis, dim):
+    count = lax.axis_size(axis)
+    pairs = [(i, (i + 1) % count) for i in range(count)]
+    back = [(b, a) for a, b in pairs]
+    lower, upper = ([], [])
+    for step in range(count - 1):
+        if step % 2 == 0:
+            lower.append(lax.ppermute(lower[-1] if lower else x, axis, pairs))
+        else:
+            upper.append(lax.ppermute(upper[-1] if upper else x, axis, back))
+    tiles = jnp.stack([*lower[::-1], x, *upper])
+    shift = lax.axis_index(axis) - len(lower)
+    tiles = tiles[(jnp.arange(count) - shift) % count]
+    return in_order(tiles, dim)
 
 
 def from_behind(array, axis, by):
@@ -93,7 +115,7 @@
     own_hot = lax.dynamic_slice_in_dim(all_hot, start, img_dev, 0)
     first_kernel, second_kernel, third_kernel = (
         lax.all_gather(first_atrous_weight, "dp", axis=2, tiled=True),
-        lax.all_gather(second_atrous_weight, "dp", axis=2, tiled=True),
+        ring_gather(second_atrous_weight, "dp", 2),
         lax.all_gather(third_atrous_weight, "dp", axis=2, tiled=True),
     )
     pointwise_output = jnp.einsum(

time: 382 us -> 354 us (0.927)
  waiting for transfers between devices: 247 us -> 167 us
  starting transfers between devices: 8.15 us -> 39.3 us
  local copies, waits for them, and re-layouts: 7.13 us -> 32.4 us
    ppermute x0 -> x15, waiting for transfers between devices: none -> 49.3 us  [the longest x8 35.6 us: ring_gather(): lower.append(lax.ppermute(lower[-1] if lower else x, axis, pairs))]
    all_gather x1, waiting for transfers between devices: 46.5 us -> 0.02 us  [shards(): lax.all_gather(first_atrous_weight, 'dp', axis=2, tiled=True)]
    all_gather x1 -> x0, waiting for transfers between devices: 42.7 us -> none  [shards(): lax.all_gather(second_atrous_weight, 'dp', axis=2, tiled=True)]
    all_gather x1, waiting for transfers between devices: 37.6 us -> 0.01 us  [shards(): lax.all_gather(third_atrous_weight, 'dp', axis=2, tiled=True)]
    ppermute x0 -> x15, starting transfers between devices: none -> 32.4 us  [the longest x7 31.8 us: ring_gather(): upper.append(lax.ppermute(upper[-1] if upper else x, axis, back))]
    unnamed x30 -> x49, local copies, waits for them, and re-layouts: 3.15 us -> 19.5 us
    gather x0 -> x1, local copies, waits for them, and re-layouts: none -> 5.32 us  [ring_gather(): tiles = tiles[(jnp.arange(count) - shift) % count]]
    dot_general x9, matrix products: 22.5 us -> 18.3 us  [row_tap_list(): jnp.einsum('irwc,kco->irwko', block_tensor, kernel_row_slice, preferred_e...]
  transfers between devices with their start and end apart: 10 -> 24, of which waited for: 4 -> 13; matrix products, arithmetic and copies ran while one was open for 10% -> 16% of each run, Pallas kernels for 0% -> 0%
where the time goes in v1:
time: 354 us; the launch traced here: 353 us
  waiting for transfers between devices  167 us (47%)
  blocking collectives  63.4 us (18%)
  starting transfers between devices  39.3 us (11%)
  local copies, waits for them, and re-layouts  32.4 us (9%)
  matrix products  26.8 us (8%)
  between operations  13.6 us (4%)
  other arithmetic  10.5 us (3%)
    psum x1, waiting for transfers between devices, shards(): lax.psum((group_first, group_second), ('dp', 'rows'))  117 us
    psum x1, blocking collectives, project(): lax.psum((group_first, group_second), ('dp', 'rows'))  41.1 us
    ppermute x8, waiting for transfers between devices, ring_gather(): lower.append(lax.ppermute(lower[-1] if lower else x, axis, pairs))  35.6 us
    ppermute x7, starting transfers between devices, ring_gather(): upper.append(lax.ppermute(upper[-1] if upper else x, axis, back))  31.8 us
    unnamed x49, local copies, waits for them, and re-layouts  19.5 us
    dot_general x9, matrix products, row_tap_list(): jnp.einsum('irwc,kco->irwko', block_tensor, kernel_row_slice, preferred_e...  18.3 us
    all_to_all x1, blocking collectives, shards(): lax.all_to_all(local_out, 'dp', split_axis=2, concat_axis=0, tiled=True)  17.3 us
    ppermute x7, waiting for transfers between devices, ring_gather(): upper.append(lax.ppermute(upper[-1] if upper else x, axis, back))  13.7 us
  transfers between devices with their start and end apart: 24, of which 13 were waited for; matrix products, arithmetic and copies ran while one was open for 16% of the time, Pallas kernels for 0%

profile of v1, /device:TPU:0, one launch (start us, length us, event | category | flops | bytes accessed | tf_op | source)
XLA Modules:
  0.0 352.7 jit_solution(4148611944452152799)
XLA Ops:
  7.8 9.6 %collective-permute-done.2 = bf16[3,3,64,256]{3,2,1,0:T(8,128)(2,1)S(1)} collective-permute-done((bf16[3,3,64,256]{3,2,1,0:T(8,128)(2,1)}, bf16[3,3,64,256]{3,2,1,0:T(8,128)(2,1)S(1)}, u32[]{:S(2)}, u32[]{:S(2)}) %collective-permute-start.2) | collective-permute-done | bytes 294944 | tf_op jit(solution)/shard_map/ppermute | solution.py:24
  17.4 4.4 %collective-permute-start.10 = (bf16[3,3,64,256]{3,2,1,0:T(8,128)(2,1)}, bf16[3,3,64,256]{3,2,1,0:T(8,128)(2,1)S(1)}, u32[]{:S(2)}, u32[]{:S(2)}) collective-permute-start(bf16[3,3,64,256]{3,2,1,0:T(8,128)(2,1)} %param.14), channel_id=1, source_target_pairs={{2,0},{4,2},{6,4},{8,6},{10,8},{12,10},{14,12},{16,14},{18,16},{20... | collective-permute-start | bytes 884744 | tf_op jit(solution)/shard_map/ppermute | solution.py:26
  21.9 5.1 %collective-permute-done.3 = bf16[3,3,64,256]{3,2,1,0:T(8,128)(2,1)S(1)} collective-permute-done((bf16[3,3,64,256]{3,2,1,0:T(8,128)(2,1)S(1)}, bf16[3,3,64,256]{3,2,1,0:T(8,128)(2,1)S(1)}, u32[]{:S(2)}, u32[]{:S(2)}) %collective-permute-start.3) | collective-permute-done | bytes 294944 | tf_op jit(solution)/shard_map/ppermute | solution.py:24
  27.4 4.6 %collective-permute-start.11 = (bf16[3,3,64,256]{3,2,1,0:T(8,128)(2,1)S(1)}, bf16[3,3,64,256]{3,2,1,0:T(8,128)(2,1)S(1)}, u32[]{:S(2)}, u32[]{:S(2)}) collective-permute-start(bf16[3,3,64,256]{3,2,1,0:T(8,128)(2,1)S(1)} %collective-permute-done.10), channel_id=1, source_target_pairs={{2,0},{4,2},{6,4},{8,6},{10,8},{12,10},{14,12},{16,14},{18,16},{20... | collective-permute-start | bytes 884744 | tf_op jit(solution)/shard_map/ppermute | solution.py:26
  32.0 6.4 %collective-permute-done.4 = bf16[3,3,64,256]{3,2,1,0:T(8,128)(2,1)S(1)} collective-permute-done((bf16[3,3,64,256]{3,2,1,0:T(8,128)(2,1)S(1)}, bf16[3,3,64,256]{3,2,1,0:T(8,128)(2,1)S(1)}, u32[]{:S(2)}, u32[]{:S(2)}) %collective-permute-start.4) | collective-permute-done | bytes 294944 | tf_op jit(solution)/shard_map/ppermute | solution.py:24
  38.4 4.4 %collective-permute-start.12 = (bf16[3,3,64,256]{3,2,1,0:T(8,128)(2,1)S(1)}, bf16[3,3,64,256]{3,2,1,0:T(8,128)(2,1)S(1)}, u32[]{:S(2)}, u32[]{:S(2)}) collective-permute-start(bf16[3,3,64,256]{3,2,1,0:T(8,128)(2,1)S(1)} %collective-permute-done.11), channel_id=1, source_target_pairs={{2,0},{4,2},{6,4},{8,6},{10,8},{12,10},{14,12},{16,14},{18,16},{20... | collective-permute-start | bytes 884744 | tf_op jit(solution)/shard_map/ppermute | solution.py:26
  42.8 4.5 %collective-permute-done.5 = bf16[3,3,64,256]{3,2,1,0:T(8,128)(2,1)S(1)} collective-permute-done((bf16[3,3,64,256]{3,2,1,0:T(8,128)(2,1)S(1)}, bf16[3,3,64,256]{3,2,1,0:T(8,128)(2,1)S(1)}, u32[]{:S(2)}, u32[]{:S(2)}) %collective-permute-start.5) | collective-permute-done | bytes 294944 | tf_op jit(solution)/shard_map/ppermute | solution.py:24
  47.3 5.9 %collective-permute-done.12 = bf16[3,3,64,256]{3,2,1,0:T(8,128)(2,1)S(1)} collective-permute-done((bf16[3,3,64,256]{3,2,1,0:T(8,128)(2,1)S(1)}, bf16[3,3,64,256]{3,2,1,0:T(8,128)(2,1)S(1)}, u32[]{:S(2)}, u32[]{:S(2)}) %collective-permute-start.12) | collective-permute-done | bytes 294944 | tf_op jit(solution)/shard_map/ppermute | solution.py:26
  53.2 4.6 %collective-permute-start.13 = (bf16[3,3,64,256]{3,2,1,0:T(8,128)(2,1)S(1)}, bf16[3,3,64,256]{3,2,1,0:T(8,128)(2,1)S(1)}, u32[]{:S(2)}, u32[]{:S(2)}) collective-permute-start(bf16[3,3,64,256]{3,2,1,0:T(8,128)(2,1)S(1)} %collective-permute-done.12), channel_id=1, source_target_pairs={{2,0},{4,2},{6,4},{8,6},{10,8},{12,10},{14,12},{16,14},{18,16},{20... | collective-permute-start | bytes 884744 | tf_op jit(solution)/shard_map/ppermute | solution.py:26
  57.8 3.4 collective-permute-done.6
  61.3 2.5 collective-permute-done.13
  63.7 4.7 %collective-permute-start.14 = (bf16[3,3,64,256]{3,2,1,0:T(8,128)(2,1)S(1)}, bf16[3,3,64,256]{3,2,1,0:T(8,128)(2,1)S(1)}, u32[]{:S(2)}, u32[]{:S(2)}) collective-permute-start(bf16[3,3,64,256]{3,2,1,0:T(8,128)(2,1)S(1)} %collective-permute-done.13), channel_id=1, source_target_pairs={{2,0},{4,2},{6,4},{8,6},{10,8},{12,10},{14,12},{16,14},{18,16},{20... | collective-permute-start | bytes 884744 | tf_op jit(solution)/shard_map/ppermute | solution.py:26
  68.4 3.4 collective-permute-done.7
  71.9 0.8 dynamic-slice
  72.7 4.9 %collective-permute-done.14 = bf16[3,3,64,256]{3,2,1,0:T(8,128)(2,1)S(1)} collective-permute-done((bf16[3,3,64,256]{3,2,1,0:T(8,128)(2,1)S(1)}, bf16[3,3,64,256]{3,2,1,0:T(8,128)(2,1)S(1)}, u32[]{:S(2)}, u32[]{:S(2)}) %collective-permute-start.14) | collective-permute-done | bytes 294944 | tf_op jit(solution)/shard_map/ppermute | solution.py:26
  77.6 4.6 %collective-permute-start.15 = (bf16[3,3,64,256]{3,2,1,0:T(8,128)(2,1)S(1)}, bf16[3,3,64,256]{3,2,1,0:T(8,128)(2,1)S(1)}, u32[]{:S(2)}, u32[]{:S(2)}) collective-permute-start(bf16[3,3,64,256]{3,2,1,0:T(8,128)(2,1)S(1)} %collective-permute-done.14), channel_id=1, source_target_pairs={{2,0},{4,2},{6,4},{8,6},{10,8},{12,10},{14,12},{16,14},{18,16},{20... | collective-permute-start | bytes 884744 | tf_op jit(solution)/shard_map/ppermute | solution.py:26
  82.2 1.5 collective-permute-done.8
  83.8 3.0 fusion.46
  86.7 4.4 %collective-permute-start.16 = (bf16[3,3,64,256]{3,2,1,0:T(8,128)(2,1)S(1)}, bf16[3,3,64,256]{3,2,1,0:T(8,128)(2,1)S(1)}, u32[]{:S(2)}, u32[]{:S(2)}) collective-permute-start(bf16[3,3,64,256]{3,2,1,0:T(8,128)(2,1)S(1)} %collective-permute-done.15), channel_id=1, source_target_pairs={{2,0},{4,2},{6,4},{8,6},{10,8},{12,10},{14,12},{16,14},{18,16},{20... | collective-permute-start | bytes 884744 | tf_op jit(solution)/shard_map/ppermute | solution.py:26
  91.2 1.7 collective-permute-done.9
  93.6 1.7 bitcast_dynamic-update-slice_fusion.14
  95.3 1.7 bitcast_dynamic-update-slice_fusion.13
  97.0 0.7 bitcast_dynamic-update-slice_fusion.12
  99.2 0.7 bitcast_dynamic-update-slice_fusion.9
  100.7 0.7 bitcast_dynamic-update-slice_fusion.7
  101.4 0.7 bitcast_dynamic-update-slice_fusion.6
  102.2 0.8 bitcast_dynamic-update-slice_fusion.5
  102.9 0.7 bitcast_dynamic-update-slice_fusion.4
  106.6 5.3 %gather_fusion = bf16[16,3,3,64,256]{4,3,2,1,0:T(8,128)(2,1)} fusion(bf16[16,3,3,64,256]{4,3,2,1,0:T(8,128)(2,1)} %bitcast_dynamic-update-slice_fusion, s32[1024]{0:T(1024)S(1)} %pad_clamp_fusion), kind=kCustom, calls=%fused_computation | custom fusion | bytes 9437248 | tf_op jit(solution)/shard_map/gather | solution.py:29
  111.9 3.4 fusion.96
  115.4 1.3 copy-done.2
  116.7 1.5 convolution_bitcast_fusion.1
  118.3 1.0 fusion.33
  120.1 1.4 convolution_bitcast_fusion
  121.6 1.0 fusion.35
  122.7 1.5 collective-permute-start.18
  124.5 5.0 %psum.37 = f32[2,1024]{1,0:T(2,128)S(1)} all-reduce(f32[2,1024]{1,0:T(2,128)S(1)} %convert_reduce_fusion), channel_id=1, replica_groups=mesh['dp'=16,'rows'=2] {'rows'}, use_global_device_ids=true, to_apply=%region_5.6 | all-reduce | flops 2048 | bytes 16384 | tf_op jit(solution)/shard_map/psum | solution.py:135
  129.6 1.3 copy-done.3
  130.9 1.4 convolution_bitcast_fusion.2
  132.5 0.8 copy-done.5
  133.4 1.7 fusion.31
  135.3 2.8 fusion.8
  138.2 1.0 fusion.25
  139.2 1.5 collective-permute-start
  140.8 2.8 fusion.7
  143.7 1.1 fusion.27
  144.8 1.5 collective-permute-start.1
  146.3 2.8 fusion.5
  149.4 0.8 collective-permute-start.19
  150.2 1.3 copy-done.15
  151.4 1.4 fusion.4
  153.8 2.8 fusion.9
  156.6 1.4 fusion.6
  158.3 1.7 fusion.23
  160.2 0.9 copy-done.1
  161.5 0.9 fusion.76
  162.4 0.9 fusion.75
  164.2 116.7 %all-reduce.22.cloned.1.call-done = (f32[8,1024]{1,0:T(8,128)}, f32[8,1024]{1,0:T(8,128)}) async-done(((f32[8,1024]{1,0:T(8,128)}, f32[8,1024]{1,0:T(8,128)}), (f32[8,1024]{1,0:T(8,128)}, f32[8,1024]{1,0:T(8,128)})) %all-reduce.22.cloned.1.call-update) | async-done | bytes 65552 | tf_op jit(solution)/shard_map/psum | solution.py:136
  280.9 1.0 fusion.55
  281.9 1.0 fusion.48
  282.9 1.7 maximum_convert_fusion
  285.9 41.1 %all-reduce.18 = (f32[8,256]{1,0:T(8,128)S(1)}, f32[8,256]{1,0:T(8,128)S(1)}) all-reduce(f32[8,256]{1,0:T(8,128)S(1)} %fusion.73, f32[8,256]{1,0:T(8,128)S(1)} %fusion.74), channel_id=1, replica_groups=mesh['dp'=16,'rows'=2] {'dp','rows'}, use_global_device_ids=true, to_apply=%region_9.10 | all-reduce | flops 4096 | bytes 32768 | tf_op jit(solution)/shard_map/psum | solution.py:85
  328.0 17.3 %all_to_all.18 = bf16[2,6,64,256]{3,0,1,2:T(2,128)(2,1)S(1)} all-to-all(bf16[2,6,64,256]{3,0,1,2:T(2,128)(2,1)S(1)} %copy.79), channel_id=1, replica_groups=mesh['dp'=16,'rows'=2] {'dp'}, dimensions={2} | all-to-all | bytes 786432 | tf_op jit(solution)/shard_map/all_to_all | solution.py:157
  345.3 0.9 copy.80
  (93 shorter events, 14.8 us)
Async XLA Ops:
  6.5 278.1 %copy-start = (bf16[1280,256]{1,0:T(8,128)(2,1)S(1)}, bf16[1280,256]{1,0:T(8,128)(2,1)}, u32[]{:S(2)}) copy-start(bf16[1280,256]{1,0:T(8,128)(2,1)} %param.18) | copy-start | bytes 1966084
  6.5 128.6 %all-gather.3.cloned.1.call-start = ((), (), s32[]{:S(2)}) async-start(), calls=%async_computation.1 | async-start | bytes 5013504 | tf_op jit(solution)/shard_map/all_gather | solution.py:117
  7.3 139.0 %all-gather.5.cloned.1.call-start = ((), (), s32[]{:S(2)}) async-start(), calls=%async_computation.2 | async-start | bytes 5013504 | tf_op jit(solution)/shard_map/all_gather | solution.py:119
  7.3 10.1 %collective-permute-start.2 = (bf16[3,3,64,256]{3,2,1,0:T(8,128)(2,1)}, bf16[3,3,64,256]{3,2,1,0:T(8,128)(2,1)S(1)}, u32[]{:S(2)}, u32[]{:S(2)}) collective-permute-start(bf16[3,3,64,256]{3,2,1,0:T(8,128)(2,1)} %param.14), channel_id=1, source_target_pairs={{0,2},{2,4},{4,6},{6,8},{8,10},{10,12},{12,14},{14,16},{16,18},{18... | collective-permute-start | bytes 884744 | tf_op jit(solution)/shard_map/ppermute | solution.py:24
  17.4 9.6 %collective-permute-start.3 = (bf16[3,3,64,256]{3,2,1,0:T(8,128)(2,1)S(1)}, bf16[3,3,64,256]{3,2,1,0:T(8,128)(2,1)S(1)}, u32[]{:S(2)}, u32[]{:S(2)}) collective-permute-start(bf16[3,3,64,256]{3,2,1,0:T(8,128)(2,1)S(1)} %collective-permute-done.2), channel_id=1, source_target_pairs={{0,2},{2,4},{4,6},{6,8},{8,10},{10,12},{12,14},{14,16},{16,18},{18... | collective-permute-start | bytes 884744 | tf_op jit(solution)/shard_map/ppermute | solution.py:24
  17.4 10.0 %collective-permute-start.10 = (bf16[3,3,64,256]{3,2,1,0:T(8,128)(2,1)}, bf16[3,3,64,256]{3,2,1,0:T(8,128)(2,1)S(1)}, u32[]{:S(2)}, u32[]{:S(2)}) collective-permute-start(bf16[3,3,64,256]{3,2,1,0:T(8,128)(2,1)} %param.14), channel_id=1, source_target_pairs={{2,0},{4,2},{6,4},{8,6},{10,8},{12,10},{14,12},{16,14},{18,16},{20... | collective-permute-start | bytes 884744 | tf_op jit(solution)/shard_map/ppermute | solution.py:26
  27.0 11.4 %collective-permute-start.4 = (bf16[3,3,64,256]{3,2,1,0:T(8,128)(2,1)S(1)}, bf16[3,3,64,256]{3,2,1,0:T(8,128)(2,1)S(1)}, u32[]{:S(2)}, u32[]{:S(2)}) collective-permute-start(bf16[3,3,64,256]{3,2,1,0:T(8,128)(2,1)S(1)} %collective-permute-done.3), channel_id=1, source_target_pairs={{0,2},{2,4},{4,6},{6,8},{8,10},{10,12},{12,14},{14,16},{16,18},{18... | collective-permute-start | bytes 884744 | tf_op jit(solution)/shard_map/ppermute | solution.py:24
  27.4 11.0 %collective-permute-start.11 = (bf16[3,3,64,256]{3,2,1,0:T(8,128)(2,1)S(1)}, bf16[3,3,64,256]{3,2,1,0:T(8,128)(2,1)S(1)}, u32[]{:S(2)}, u32[]{:S(2)}) collective-permute-start(bf16[3,3,64,256]{3,2,1,0:T(8,128)(2,1)S(1)} %collective-permute-done.10), channel_id=1, source_target_pairs={{2,0},{4,2},{6,4},{8,6},{10,8},{12,10},{14,12},{16,14},{18,16},{20... | collective-permute-start | bytes 884744 | tf_op jit(solution)/shard_map/ppermute | solution.py:26
  38.4 8.9 %collective-permute-start.5 = (bf16[3,3,64,256]{3,2,1,0:T(8,128)(2,1)S(1)}, bf16[3,3,64,256]{3,2,1,0:T(8,128)(2,1)S(1)}, u32[]{:S(2)}, u32[]{:S(2)}) collective-permute-start(bf16[3,3,64,256]{3,2,1,0:T(8,128)(2,1)S(1)} %collective-permute-done.4), channel_id=1, source_target_pairs={{0,2},{2,4},{4,6},{6,8},{8,10},{10,12},{12,14},{14,16},{16,18},{18... | collective-permute-start | bytes 884744 | tf_op jit(solution)/shard_map/ppermute | solution.py:24
  38.4 14.9 %collective-permute-start.12 = (bf16[3,3,64,256]{3,2,1,0:T(8,128)(2,1)S(1)}, bf16[3,3,64,256]{3,2,1,0:T(8,128)(2,1)S(1)}, u32[]{:S(2)}, u32[]{:S(2)}) collective-permute-start(bf16[3,3,64,256]{3,2,1,0:T(8,128)(2,1)S(1)} %collective-permute-done.11), channel_id=1, source_target_pairs={{2,0},{4,2},{6,4},{8,6},{10,8},{12,10},{14,12},{16,14},{18,16},{20... | collective-permute-start | bytes 884744 | tf_op jit(solution)/shard_map/ppermute | solution.py:26
  47.3 14.0 %collective-permute-start.6 = (bf16[3,3,64,256]{3,2,1,0:T(8,128)(2,1)S(1)}, bf16[3,3,64,256]{3,2,1,0:T(8,128)(2,1)S(1)}, u32[]{:S(2)}, u32[]{:S(2)}) collective-permute-start(bf16[3,3,64,256]{3,2,1,0:T(8,128)(2,1)S(1)} %collective-permute-done.5), channel_id=1, source_target_pairs={{0,2},{2,4},{4,6},{6,8},{8,10},{10,12},{12,14},{14,16},{16,18},{18... | collective-permute-start | bytes 884744 | tf_op jit(solution)/shard_map/ppermute | solution.py:24
  53.2 10.5 %collective-permute-start.13 = (bf16[3,3,64,256]{3,2,1,0:T(8,128)(2,1)S(1)}, bf16[3,3,64,256]{3,2,1,0:T(8,128)(2,1)S(1)}, u32[]{:S(2)}, u32[]{:S(2)}) collective-permute-start(bf16[3,3,64,256]{3,2,1,0:T(8,128)(2,1)S(1)} %collective-permute-done.12), channel_id=1, source_target_pairs={{2,0},{4,2},{6,4},{8,6},{10,8},{12,10},{14,12},{16,14},{18,16},{20... | collective-permute-start | bytes 884744 | tf_op jit(solution)/shard_map/ppermute | solution.py:26
  61.3 2.5 copy-start.8
  61.3 10.5 %collective-permute-start.7 = (bf16[3,3,64,256]{3,2,1,0:T(8,128)(2,1)S(1)}, bf16[3,3,64,256]{3,2,1,0:T(8,128)(2,1)}, u32[]{:S(2)}, u32[]{:S(2)}) collective-permute-start(bf16[3,3,64,256]{3,2,1,0:T(8,128)(2,1)S(1)} %collective-permute-done.6), channel_id=1, source_target_pairs={{0,2},{2,4},{4,6},{6,8},{8,10},{10,12},{12,14},{14,16},{16,18},{18... | collective-permute-start | bytes 884744 | tf_op jit(solution)/shard_map/ppermute | solution.py:24
  63.7 13.9 %collective-permute-start.14 = (bf16[3,3,64,256]{3,2,1,0:T(8,128)(2,1)S(1)}, bf16[3,3,64,256]{3,2,1,0:T(8,128)(2,1)S(1)}, u32[]{:S(2)}, u32[]{:S(2)}) collective-permute-start(bf16[3,3,64,256]{3,2,1,0:T(8,128)(2,1)S(1)} %collective-permute-done.13), channel_id=1, source_target_pairs={{2,0},{4,2},{6,4},{8,6},{10,8},{12,10},{14,12},{16,14},{18,16},{20... | collective-permute-start | bytes 884744 | tf_op jit(solution)/shard_map/ppermute | solution.py:26
  71.8 12.0 %collective-permute-start.8 = (bf16[3,3,64,256]{3,2,1,0:T(8,128)(2,1)}, bf16[3,3,64,256]{3,2,1,0:T(8,128)(2,1)}, u32[]{:S(2)}, u32[]{:S(2)}) collective-permute-start(bf16[3,3,64,256]{3,2,1,0:T(8,128)(2,1)} %collective-permute-done.7), channel_id=1, source_target_pairs={{0,2},{2,4},{4,6},{6,8},{8,10},{10,12},{12,14},{14,16},{16,18},{18... | collective-permute-start | bytes 884744 | tf_op jit(solution)/shard_map/ppermute | solution.py:24
  71.8 209.1 %all-reduce.22.cloned.1.call-start = ((), (), s32[]{:S(2)}) async-start(), calls=%async_computation.3 | async-start | bytes 131072 | tf_op jit(solution)/shard_map/psum | solution.py:136
  71.9 25.2 %copy-start.9 = (bf16[3,3,64,256]{3,2,1,0:T(8,128)(2,1)S(1)}, bf16[3,3,64,256]{3,2,1,0:T(8,128)(2,1)}, u32[]{:S(2)}) copy-start(bf16[3,3,64,256]{3,2,1,0:T(8,128)(2,1)} %copy-done.8) | copy-start | bytes 884740
  72.7 89.7 %copy-start.13 = (s32[2]{0:T(128)}, s32[2]{0:T(128)S(1)}, u32[]{:S(2)}) copy-start(s32[2]{0:T(128)S(1)} %dynamic-slice) | copy-start | bytes 28
  77.6 9.1 %collective-permute-start.15 = (bf16[3,3,64,256]{3,2,1,0:T(8,128)(2,1)S(1)}, bf16[3,3,64,256]{3,2,1,0:T(8,128)(2,1)S(1)}, u32[]{:S(2)}, u32[]{:S(2)}) collective-permute-start(bf16[3,3,64,256]{3,2,1,0:T(8,128)(2,1)S(1)} %collective-permute-done.14), channel_id=1, source_target_pairs={{2,0},{4,2},{6,4},{8,6},{10,8},{12,10},{14,12},{16,14},{18,16},{20... | collective-permute-start | bytes 884744 | tf_op jit(solution)/shard_map/ppermute | solution.py:26
  83.7 9.2 %collective-permute-start.9 = (bf16[3,3,64,256]{3,2,1,0:T(8,128)(2,1)}, bf16[3,3,64,256]{3,2,1,0:T(8,128)(2,1)S(1)}, u32[]{:S(2)}, u32[]{:S(2)}) collective-permute-start(bf16[3,3,64,256]{3,2,1,0:T(8,128)(2,1)} %collective-permute-done.8), channel_id=1, source_target_pairs={{0,2},{2,4},{4,6},{6,8},{8,10},{10,12},{12,14},{14,16},{16,18},{18... | collective-permute-start | bytes 884744 | tf_op jit(solution)/shard_map/ppermute | solution.py:24
  86.7 13.9 %copy-start.7 = (bf16[3,3,64,256]{3,2,1,0:T(8,128)(2,1)S(1)}, bf16[3,3,64,256]{3,2,1,0:T(8,128)(2,1)}, u32[]{:S(2)}) copy-start(bf16[3,3,64,256]{3,2,1,0:T(8,128)(2,1)} %param.14) | copy-start | bytes 884740
  86.7 19.1 %collective-permute-start.16 = (bf16[3,3,64,256]{3,2,1,0:T(8,128)(2,1)S(1)}, bf16[3,3,64,256]{3,2,1,0:T(8,128)(2,1)S(1)}, u32[]{:S(2)}, u32[]{:S(2)}) collective-permute-start(bf16[3,3,64,256]{3,2,1,0:T(8,128)(2,1)S(1)} %collective-permute-done.15), channel_id=1, source_target_pairs={{2,0},{4,2},{6,4},{8,6},{10,8},{12,10},{14,12},{16,14},{18,16},{20... | collective-permute-start | bytes 884744 | tf_op jit(solution)/shard_map/ppermute | solution.py:26
  115.3 1.4 copy-start.2
  119.3 13.3 %collective-permute-start.17 = (f32[2,6,64,256]{3,2,1,0:T(8,128)}, f32[2,6,64,256]{3,2,1,0:T(8,128)S(1)}, u32[]{:S(2)}, u32[]{:S(2)}) collective-permute-start(f32[2,6,64,256]{3,2,1,0:T(8,128)} %fusion.33), channel_id=1, source_target_pairs={} | collective-permute-start | bytes 2359304 | tf_op jit(solution)/shard_map/ppermute | solution.py:36
  122.7 9.9 %collective-permute-start.18 = (f32[2,6,64,256]{3,2,1,0:T(8,128)}, f32[2,6,64,256]{3,2,1,0:T(8,128)}, u32[]{:S(2)}, u32[]{:S(2)}) collective-permute-start(f32[2,6,64,256]{3,2,1,0:T(8,128)} %fusion.35), channel_id=1, source_target_pairs={} | collective-permute-start | bytes 2359304 | tf_op jit(solution)/shard_map/ppermute | solution.py:36
  129.5 1.4 copy-start.3
  132.5 0.9 copy-start.5
  133.4 1.9 copy-start.4
  139.2 19.1 %collective-permute-start = (f32[2,6,64,256]{3,2,1,0:T(8,128)}, f32[2,6,64,256]{3,2,1,0:T(8,128)}, u32[]{:S(2)}, u32[]{:S(2)}) collective-permute-start(f32[2,6,64,256]{3,2,1,0:T(8,128)} %fusion.25), channel_id=1, source_target_pairs={} | collective-permute-start | bytes 2359304 | tf_op jit(solution)/shard_map/ppermute | solution.py:36
  144.8 13.5 %collective-permute-start.1 = (f32[2,6,64,256]{3,2,1,0:T(8,128)}, f32[2,6,64,256]{3,2,1,0:T(8,128)}, u32[]{:S(2)}, u32[]{:S(2)}) collective-permute-start(f32[2,6,64,256]{3,2,1,0:T(8,128)} %fusion.27), channel_id=1, source_target_pairs={} | collective-permute-start | bytes 2359304 | tf_op jit(solution)/shard_map/ppermute | solution.py:36
  149.1 2.3 copy-start.15
  149.4 10.6 %collective-permute-start.19 = (f32[2,6,64,256]{3,2,1,0:T(8,128)S(1)}, f32[2,6,64,256]{3,2,1,0:T(8,128)S(1)}, u32[]{:S(2)}, u32[]{:S(2)}) collective-permute-start(f32[2,6,64,256]{3,2,1,0:T(8,128)S(1)} %fusion.41), channel_id=1, source_target_pairs={} | collective-permute-start | bytes 2359304 | tf_op jit(solution)/shard_map/ppermute | solution.py:36
  153.1 6.9 %collective-permute-start.20 = (f32[2,6,64,256]{3,2,1,0:T(8,128)S(1)}, f32[2,6,64,256]{3,2,1,0:T(8,128)S(1)}, u32[]{:S(2)}, u32[]{:S(2)}) collective-permute-start(f32[2,6,64,256]{3,2,1,0:T(8,128)S(1)} %fusion.43), channel_id=1, source_target_pairs={} | collective-permute-start | bytes 2359304 | tf_op jit(solution)/shard_map/ppermute | solution.py:36
  160.0 1.1 copy-start.1
  161.1 2.2 copy-start.6
  161.1 2.4 copy-start.10
  284.7 0.7 copy-start.14
  284.7 42.7 %copy-start.11 = (f32[256]{0:T(256)S(1)}, f32[256]{0:T(256)}, u32[]{:S(2)}) copy-start(f32[256]{0:T(256)} %param.22) | copy-start | bytes 3076
  284.7 42.7 %copy-start.12 = (f32[256]{0:T(256)S(1)}, f32[256]{0:T(256)}, u32[]{:S(2)}) copy-start(f32[256]{0:T(256)} %param.21) | copy-start | bytes 3076
Sparse Core Ops, SparseCore 0:
  9.5 72.7 all-gather.2
  84.5 54.8 all-gather.4
  163.4 117.4 all-reduce.21
